TPU v7x, 32 devices: a whole 2x2x4 slice. The times are simulated.
32 devices in a mesh: row: 8 (over y, x, core), col: 4 (over z).
Axes of the slice: x: 2, y: 2, z: 4, core: 2. Of those that a mesh axis runs over, the one named last changes fastest.
Arguments:
- inverse_blocks: float32 [4096, 4096], P('row', 'col'), may hold values from -0.09375 to 0.09375
- panel: bfloat16 [4096, 4096], P('row', 'col'), may hold values from -1.5 to 1.5
- diag_inverse: float32 [512, 4096], P('row', 'col'), may hold values from -6 to 6
- members: int32 [8, 8], replicated, may hold values from 0 to 7, each once within a row
- counts: int32 [8], replicated, may hold values from 1 to 8, as said below
Outputs:
- offdiag: float32 [4096, 4096], P('row', 'col')
- new_diag: float32 [512, 4096], P('row', 'col')
Inputs may be any that keep to these rules, and one draw needn't show every extreme that they name: Each row of members names every ancestor once. `counts`: some supernode lists all 8 ancestors and some lists one.
All inputs are finite; a program needn't handle non-finite values.
Results may differ from a plain program's by a relative error of at most 0.0003.
Values may be sent and summed in bfloat16 or wider, within the bound.
A program may use at most 128 MiB of HBM per device.

v0:
```python
import jax
import jax.numpy as jnp
from jax import lax
from jax.sharding import PartitionSpec as P

B = 512


def body(inverse_blocks, panel, diag_inverse, members, counts):
    rows_dev = panel.shape[0]
    sup_count = panel.shape[1] // B
    row_index = lax.axis_index("row")
    col_index = lax.axis_index("col")
    ancestor = row_index * rows_dev // B
    first_sup = col_index * sup_count
    local_members = lax.dynamic_slice_in_dim(members, first_sup, sup_count, 0)
    local_counts = lax.dynamic_slice_in_dim(counts, first_sup, sup_count, 0)
    slot_index = jnp.arange(members.shape[1], dtype=jnp.int32)
    live_slot = slot_index[None, :] < local_counts[:, None]
    row_mask = jnp.sum(
        jnp.where((local_members == ancestor) & live_slot, 1.0, 0.0).astype(jnp.float32), axis=1
    )
    column_mask = jnp.repeat(row_mask, B)
    masked = panel * column_mask.astype(jnp.bfloat16)[None, :]
    inverse_rows = lax.all_gather(inverse_blocks, "col", axis=1, tiled=True)
    running = jnp.dot(
        inverse_rows,
        lax.all_gather(masked, "row", axis=0, tiled=True).astype(jnp.float32),
        precision=lax.Precision.HIGHEST,
    )
    offdiag = -(running * column_mask[None, :])
    masked_wide = masked.astype(jnp.float32).reshape(rows_dev, sup_count, B)
    offdiag_wide = offdiag.reshape(rows_dev, sup_count, B)
    diag_terms = jnp.einsum(
        "ikc,ikd->ckd", masked_wide, offdiag_wide, precision=lax.Precision.HIGHEST
    )
    summed = lax.psum_scatter(
        diag_terms.reshape(B, sup_count * B), "row", scatter_dimension=0, tiled=True
    )
    return (offdiag, diag_inverse - summed)


def solution(mesh):
    return jax.shard_map(
        body,
        mesh=mesh,
        in_specs=(P("row", "col"), P("row", "col"), P("row", "col"), P(), P()),
        out_specs=(P("row", "col"), P("row", "col")),
        check_vma=False,
    )
```

profile of v0, /device:TPU:0, one launch (start us, length us, event | category | flops | bytes accessed | tf_op | source)
XLA Modules:
  0.0 291.6 jit_solution(4853133798508175931)
XLA Ops:
  7.2 0.0 copy-start.3
  7.2 0.0 copy-start.1
  7.2 0.0 all-gather.5.cloned.1.call-start
  7.2 0.7 all-gather.5.cloned.1.call-update
  7.9 0.0 all-gather.3.cloned.1.call-start
  8.0 0.0 copy-done.3
  8.0 0.1 dynamic_slice.7
  8.1 0.9 fusion.3
  8.9 0.1 broadcast_bitcast_fusion
  9.0 0.0 copy-done.1
  9.0 1.0 broadcast_multiply_fusion
  10.1 0.0 all-gather.3.cloned.1.call-update
  10.1 0.0 copy-start
  10.1 0.0 reduce-scatter.2.cloned.1.call-start
  10.2 151.8 %all-gather.5.cloned.1.call-done = f32[512,4096]{1,0:T(8,128)} async-done(((f32[512,1024]{1,0:T(8,128)}), f32[512,4096]{1,0:T(8,128)}) %all-gather.5.cloned.1.call-update) | async-done | bytes 8388624 | tf_op jit(solution)/shard_map/all_gather | solution.py:25
  162.0 55.1 %all-gather.3.cloned.1.call-done = bf16[4096,1024]{1,0:T(8,128)(2,1)} async-done(((bf16[512,1024]{1,0:T(8,128)(2,1)}), bf16[4096,1024]{1,0:T(8,128)(2,1)}) %all-gather.3.cloned.1.call-update) | async-done | bytes 8388624 | tf_op jit(solution)/shard_map/all_gather | solution.py:28
  217.0 18.9 %multiply_negate_fusion = f32[1024,512]{1,0:T(8,128)S(1)} fusion(bf16[4096,1024]{1,0:T(8,128)(2,1)} %all-gather.3.cloned.1.call-done, f32[512,4096]{1,0:T(8,128)} %all-gather.5.cloned.1.call-done, f32[1024]{0:T(1024)S(1)} %bitcast.21), kind=kOutput, calls=%fused_computation | convolution fusion | flops 25770852352 | bytes 18878464 | tf_op jit(solution)/shard_map/dot_general | solution.py:26
  235.9 0.0 copy-done
  235.9 3.1 %fusion = f32[2,512,512]{2,1,0:T(8,128)} fusion(f32[512,2,512]{0,2,1:T(8,128)S(1)} %bitcast.17, bf16[64,2,8,512]{3,2,1,0:T(8,128)(2,1)S(1)} %bitcast.16), kind=kOutput, calls=%fused_computation.1 | convolution fusion | flops 3221225472 | bytes 5242880 | tf_op jit(solution)/shard_map/ikc,ikd->ckd/dot_general | solution.py:34
  239.0 2.9 %copy.8 = f32[512,1024]{1,0:T(8,128)} copy(f32[512,1024]{0,1:T(8,128)} %bitcast.19) | data formatting | bytes 4194304 | tf_op jit(solution)/shard_map/reshape | solution.py:38
  242.0 0.0 reduce-scatter.2.cloned.1.call-update
  242.0 0.0 copy-start.2
  242.0 1.8 copy.9
  243.8 39.6 %reduce-scatter.2.cloned.1.call-done = f32[64,1024]{1,0:T(8,128)} async-done(((f32[512,1024]{1,0:T(8,128)}), f32[64,1024]{1,0:T(8,128)}) %reduce-scatter.2.cloned.1.call-update) | async-done | bytes 262160 | tf_op jit(solution)/shard_map/reduce_scatter | solution.py:37
  283.4 0.0 copy-done.2
  283.4 1.7 sub.8
  (2 shorter events, 0.0 us)
Async XLA Ops:
  7.2 0.8 copy-start.3
  7.2 1.9 copy-start.1
  7.2 154.8 %all-gather.5.cloned.1.call-start = ((), (), s32[]{:S(2)}) async-start(), calls=%async_computation.2 | async-start | bytes 10485760 | tf_op jit(solution)/shard_map/all_gather | solution.py:25
  7.9 209.1 %all-gather.3.cloned.1.call-start = ((), (), s32[]{:S(2)}) async-start(), calls=%async_computation.1 | async-start | bytes 9437184 | tf_op jit(solution)/shard_map/all_gather | solution.py:28
  10.1 225.8 %copy-start = (bf16[512,1024]{1,0:T(8,128)(2,1)S(1)}, bf16[512,1024]{1,0:T(8,128)(2,1)}, u32[]{:S(2)}) copy-start(bf16[512,1024]{1,0:T(8,128)(2,1)} %broadcast_multiply_fusion) | copy-start | bytes 3145732
  10.1 273.3 %reduce-scatter.2.cloned.1.call-start = ((), (), s32[]{:S(2)}) async-start(), calls=%async_computation.3 | async-start | bytes 2359296 | tf_op jit(solution)/shard_map/reduce_scatter | solution.py:37
  242.0 41.4 %copy-start.2 = (f32[64,1024]{1,0:T(8,128)S(1)}, f32[64,1024]{1,0:T(8,128)}, u32[]{:S(2)}) copy-start(f32[64,1024]{1,0:T(8,128)} %param.7) | copy-start | bytes 786436
Sparse Core Ops, SparseCore 0:
  9.6 152.3 all-gather.4
  164.4 52.5 all-gather.2
  242.1 41.2 reduce-scatter.1
where the time goes:
time: 292 us
  waiting for transfers between devices  247 us (85%)
  matrix products  22 us (8%)
  between operations  13.8 us (5%)
  local copies, waits for them, and re-layouts  4.93 us (2%)
  other arithmetic  3.6 us (1%)
    all_gather x1, waiting for transfers between devices, body(): inverse_rows = lax.all_gather(inverse_blocks, 'col', axis=1, tiled=True)  152 us
    all_gather x1, waiting for transfers between devices, body(): lax.all_gather(masked, 'row', axis=0, tiled=True).astype(jnp.float32)  55.1 us
    reduce_scatter x1, waiting for transfers between devices, body(): lax.psum_scatter(diag_terms.reshape(B, sup_count * B), 'row', scatter_dim...  39.6 us
    dot_general x1, matrix products, body(): jnp.dot(inverse_rows, lax.all_gather(masked, 'row', axis=0, tiled=True).a...  18.9 us
  transfers between devices with their start and end apart: 3, of which 3 were waited for; matrix products, arithmetic and copies ran while one was open for 1% of the time, Pallas kernels for 0%

commit v1 on v0

--- a/solution.py
+++ b/solution.py
@@ -4,6 +4,30 @@
 from jax.sharding import PartitionSpec as P
 
 B = 512
+
+
+def answer_the_tables(message, at_axis):
+    message = jnp.moveaxis(message, 0, at_axis)
+    tmp = message.shape
+    return message.reshape(*tmp[:at_axis], tmp[at_axis] * tmp[at_axis + 1], *tmp[at_axis + 2 :])
+
+
+def start_limits(x_in, net_axis):
+    part_now, u_next = (lax.psum(1, axis_name=net_axis), lax.axis_index(net_axis))
+    opened, z = (x_in[None], 1)
+    while z < part_now:
+        column = []
+        for pp in [*range(part_now)]:
+            column.append((pp, pp ^ z))
+        after = lax.ppermute(opened, axis_name=net_axis, perm=column)
+        r_now = u_next & z == 0
+        opened = jnp.concatenate([jnp.where(r_now, opened, after), jnp.where(r_now, after, opened)])
+        z *= 2
+    return opened
+
+
+def bind_the_copies(slab_in, row_dim, view):
+    return answer_the_tables(start_limits(view, slab_in), row_dim)
 
 
 def body(inverse_blocks, panel, diag_inverse, members, counts):
@@ -22,7 +46,7 @@
     )
     column_mask = jnp.repeat(row_mask, B)
     masked = panel * column_mask.astype(jnp.bfloat16)[None, :]
-    inverse_rows = lax.all_gather(inverse_blocks, "col", axis=1, tiled=True)
+    inverse_rows = bind_the_copies("col", 1, inverse_blocks)
     running = jnp.dot(
         inverse_rows,
         lax.all_gather(masked, "row", axis=0, tiled=True).astype(jnp.float32),

time: 292 us -> 334 us (1.14)
  waiting for transfers between devices: 247 us -> 268 us
  other arithmetic: 3.6 us -> 19.2 us
  starting transfers between devices: 0.12 us -> 5.92 us
    ppermute x0 -> x2, waiting for transfers between devices: none -> 226 us  [start_limits(): after = lax.ppermute(opened, axis_name=net_axis, perm=column)]
    all_gather x1 -> x0, waiting for transfers between devices: 152 us -> none  [body(): inverse_rows = lax.all_gather(inverse_blocks, 'col', axis=1, tiled=True)]
    all_gather x1, waiting for transfers between devices: 55.1 us -> 0.01 us  [body(): lax.all_gather(masked, 'row', axis=0, tiled=True).astype(jnp.float32)]
    select_n x0 -> x2, other arithmetic: none -> 7.5 us  [start_limits(): jnp.where(r_now, opened, after)]
    concatenate x0 -> x2, other arithmetic: none -> 6.86 us  [start_limits(): jnp.concatenate([jnp.where(r_now, opened, after), jnp.where(r_now, after,...]
    ppermute x0 -> x2, starting transfers between devices: none -> 5.84 us  [start_limits(): after = lax.ppermute(opened, axis_name=net_axis, perm=column)]
  transfers between devices with their start and end apart: 3 -> 4, of which waited for: 3 -> 3; matrix products, arithmetic and copies ran while one was open for 1% -> 5% of each run, Pallas kernels for 0% -> 0%
where the time goes in v1:
time: 334 us
  waiting for transfers between devices  268 us (80%)
  matrix products  19.7 us (6%)
  other arithmetic  19.2 us (6%)
  between operations  14.1 us (4%)
  local copies, waits for them, and re-layouts  6.62 us (2%)
  starting transfers between devices  5.92 us (2%)
    ppermute x2, waiting for transfers between devices, start_limits(): after = lax.ppermute(opened, axis_name=net_axis, perm=column)  226 us
    reduce_scatter x1, waiting for transfers between devices, body(): lax.psum_scatter(diag_terms.reshape(B, sup_count * B), 'row', scatter_dim...  42.4 us
    dot_general x1, matrix products, body(): jnp.dot(inverse_rows, lax.all_gather(masked, 'row', axis=0, tiled=True).a...  16.3 us
    select_n x2, other arithmetic, start_limits(): jnp.where(r_now, opened, after)  7.5 us
    concatenate x2, other arithmetic, start_limits(): jnp.concatenate([jnp.where(r_now, opened, after), jnp.where(r_now, after,...  6.86 us
  transfers between devices with their start and end apart: 4, of which 3 were waited for; matrix products, arithmetic and copies ran while one was open for 5% of the time, Pallas kernels for 0%

profile of v1, /device:TPU:0, one launch (start us, length us, event | category | flops | bytes accessed | tf_op | source)
XLA Modules:
  0.0 333.8 jit_solution(3769213131975449187)
XLA Ops:
  7.2 0.0 all-gather.2.cloned.1.call-start
  7.2 0.7 dynamic_slice.7
  8.0 0.9 fusion.3
  8.8 0.1 broadcast_bitcast_fusion
  8.9 2.3 broadcast_multiply_fusion
  11.2 0.0 all-gather.2.cloned.1.call-update
  11.2 0.0 reduce-scatter.2.cloned.1.call-start
  11.3 1.9 copy.10
  13.2 0.0 copy-start.2
  13.2 3.1 collective-permute-start
  16.3 0.0 copy-done.2
  16.3 45.7 %collective-permute-done = f32[1,512,1024]{1,2,0:T(8,128)} collective-permute-done((f32[1,512,1024]{1,2,0:T(8,128)S(1)}, f32[1,512,1024]{1,2,0:T(8,128)}, u32[]{:S(2)}, u32[]{:S(2)}) %collective-permute-start) | collective-permute-done | bytes 2097184 | tf_op jit(solution)/shard_map/ppermute | solution.py:22
  62.0 2.8 broadcast_select_fusion.3
  64.8 0.0 copy-start
  64.8 2.7 pad_maximum_fusion.1
  67.5 0.0 copy-done
  67.5 2.8 collective-permute-start.1
  70.2 180.1 %collective-permute-done.1 = f32[2,512,1024]{1,2,0:T(8,128)} collective-permute-done((f32[2,512,1024]{1,2,0:T(8,128)}, f32[2,512,1024]{1,2,0:T(8,128)}, u32[]{:S(2)}, u32[]{:S(2)}) %collective-permute-start.1) | collective-permute-done | bytes 4194336 | tf_op jit(solution)/shard_map/ppermute | solution.py:22
  250.3 4.7 %broadcast_select_fusion.1 = (f32[2,512,1024]{1,2,0:T(8,128)S(1)}, f32[2,512,1024]{1,2,0:T(8,128)S(1)}) fusion(f32[2,512,1024]{1,2,0:T(8,128)} %collective-permute-done.1, pred[]{:T(512)S(6)} %eq.12, f32[1,512,1024]{1,2,0:T(8,128)} %copy-done, f32[1,512,1024]{1,2,0:T(8,128)S(1)} %get-tuple-element.4), kind=kLoop, calls=%fused_computation.4 | loop fusion | flops 3145728 | bytes 16777216 | tf_op jit(solution)/shard_map/jit(_where)/select_n | solution.py:24
  255.1 4.2 %pad_maximum_fusion = f32[4,512,1024]{1,2,0:T(8,128)} fusion(f32[2,512,1024]{1,2,0:T(8,128)S(1)} %get-tuple-element.3, f32[2,512,1024]{1,2,0:T(8,128)S(1)} %get-tuple-element.2), kind=kLoop, calls=%fused_computation | loop fusion | flops 2097152 | bytes 16777216 | tf_op jit(solution)/shard_map/concatenate | solution.py:24
  259.3 0.0 all-gather.2.cloned.1.call-done
  259.3 16.3 %multiply_negate_fusion = f32[512,1024]{1,0:T(8,128)S(1)} fusion(f32[512,4096]{0,1:T(8,128)} %bitcast.21, bf16[4096,1024]{1,0:T(8,128)(2,1)} %all-gather.2.cloned.1.call-done, f32[1024]{0:T(1024)S(1)} %bitcast.26), kind=kOutput, calls=%fused_computation.2 | convolution fusion | flops 25770852352 | bytes 18878464 | tf_op jit(solution)/shard_map/dot_general | solution.py:50
  275.6 0.0 copy-start.3
  275.6 0.0 copy-start.1
  275.6 1.9 copy.14
  277.5 0.1 copy-done.3
  277.6 0.0 copy-done.1
  277.6 3.4 %fusion = f32[2,512,512]{2,1,0:T(8,128)S(1)} fusion(f32[512,2,512]{0,2,1:T(8,128)} %bitcast.23, bf16[64,2,8,512]{3,2,1,0:T(8,128)(2,1)S(1)} %bitcast.20), kind=kOutput, calls=%fused_computation.5 | convolution fusion | flops 3221225472 | bytes 5242880 | tf_op jit(solution)/shard_map/ikc,ikd->ckd/dot_general | solution.py:58
  281.0 0.0 copy-start.4
  281.0 1.9 copy.13
  282.9 0.0 reduce-scatter.2.cloned.1.call-update
  282.9 42.4 %reduce-scatter.2.cloned.1.call-done = f32[64,1024]{1,0:T(8,128)} async-done(((f32[512,1024]{1,0:T(8,128)}), f32[64,1024]{1,0:T(8,128)}) %reduce-scatter.2.cloned.1.call-update) | async-done | bytes 262160 | tf_op jit(solution)/shard_map/reduce_scatter | solution.py:61
  325.3 0.0 copy-done.4
  325.3 1.7 sub.8
  (2 shorter events, 0.0 us)
Async XLA Ops:
  7.2 252.1 %all-gather.2.cloned.1.call-start = ((), (), s32[]{:S(2)}) async-start(), calls=%async_computation.1 | async-start | bytes 9437184 | tf_op jit(solution)/shard_map/all_gather | solution.py:52
  11.2 314.1 %reduce-scatter.2.cloned.1.call-start = ((), (), s32[]{:S(2)}) async-start(), calls=%async_computation.2 | async-start | bytes 2359296 | tf_op jit(solution)/shard_map/reduce_scatter | solution.py:61
  13.2 3.1 copy-start.2
  13.2 48.8 %collective-permute-start = (f32[1,512,1024]{1,2,0:T(8,128)S(1)}, f32[1,512,1024]{1,2,0:T(8,128)}, u32[]{:S(2)}, u32[]{:S(2)}) collective-permute-start(f32[1,512,1024]{1,2,0:T(8,128)S(1)} %bitcast.24), channel_id=1, source_target_pairs={{0,1},{1,0},{2,3},{3,2},{4,5},{5,4},{6,7},{7,6},{8,9},{9,8},{10,11... | collective-permute-start | bytes 6291464 | tf_op jit(solution)/shard_map/ppermute | solution.py:22
  64.8 2.7 copy-start
  67.5 182.9 %collective-permute-start.1 = (f32[2,512,1024]{1,2,0:T(8,128)}, f32[2,512,1024]{1,2,0:T(8,128)}, u32[]{:S(2)}, u32[]{:S(2)}) collective-permute-start(f32[2,512,1024]{1,2,0:T(8,128)} %pad_maximum_fusion.1), channel_id=1, source_target_pairs={{0,2},{1,3},{2,0},{3,1},{4,6},{5,7},{6,4},{7,5},{8,10},{9,11},{10,... | collective-permute-start | bytes 12582920 | tf_op jit(solution)/shard_map/ppermute | solution.py:22
  275.6 2.0 copy-start.3
  275.6 2.0 copy-start.1
  281.0 44.3 %copy-start.4 = (f32[64,1024]{1,0:T(8,128)S(1)}, f32[64,1024]{1,0:T(8,128)}, u32[]{:S(2)}) copy-start(f32[64,1024]{1,0:T(8,128)} %param.7) | copy-start | bytes 786436
Sparse Core Ops, SparseCore 0:
  11.3 57.0 all-gather.1
  283.0 42.2 reduce-scatter.1
